TPU v7x, 32 devices: a whole 2x2x4 slice. The times are simulated.
32 devices in a mesh: group: 2 (over core), dp: 4 (over z), section: 2 (over x), tensor: 2 (over y).
Axes of the slice: x: 2, y: 2, z: 4, core: 2. Of those that a mesh axis runs over, the one named last changes fastest.
Arguments:
- merged: bfloat16 [768, 5120], P('dp'), may hold values from -6 to 6
- counts: int32 [8], P('dp'), may hold values from 4 to 384
- owners: int32 [768, 1], P('dp'), may hold values from 0 to 3; in each aligned block of 192 rows (0 to 191, 192 to 383, ...) at most 96 rows name the same one
- w_merge: bfloat16 [5120, 8192], P(None, ('group', 'section', 'tensor')), may hold values from -0.078125 to 0.078125
- norm_gain: float32 [8192], P(('group', 'section', 'tensor')), may hold values from 0.25 to 1.75
- cotangent: bfloat16 [4, 4, 96, 8192], P('dp', None, None, ('group', 'section', 'tensor')), may hold values from -6 to 6
Outputs:
- embedded: bfloat16 [4, 4, 96, 8192], P('dp', None, None, ('group', 'section', 'tensor'))
- grad_merged: float32 [768, 5120], P('dp', ('group', 'section', 'tensor'))
- grad_weight: float32 [5120, 8192], P('dp', ('group', 'section', 'tensor'))
Inputs may be any that keep to these rules, and one draw needn't show every extreme that they name: `owners`: in each replica's 192 rows no owner appears more than 96 times.
All inputs are finite; a program needn't handle non-finite values.
Results may differ from a plain program's by a relative error of at most 0.0049.
Values may be sent and summed in bfloat16 or wider, within the bound.
A program may use at most 64 MiB of HBM per device.

v0:
```python
import jax
import jax.numpy as jnp
from jax import lax
from jax.sharding import PartitionSpec as P

D = 8192


def on_device(merged, counts, owners, w_merge, norm_gain, cotangent):
    rows = merged.shape[0]
    columns = w_merge.shape[1]
    replicas = lax.axis_size("dp")
    slots = cotangent.shape[2]
    images = counts.shape[0]
    per_image = rows // images
    projected = jnp.dot(merged, w_merge, preferred_element_type=jnp.float32).astype(jnp.bfloat16)
    row_index = jnp.arange(rows, dtype=jnp.int32)
    image_of = row_index // per_image
    picked = image_of[:, None] == jnp.arange(images, dtype=jnp.int32)[None, :]
    count_of = jnp.sum(jnp.where(picked, counts[None, :], 0), axis=1)
    valid = (4 * (row_index % per_image) < count_of).astype(jnp.float32)
    masked = (projected.astype(jnp.float32) * valid[:, None]).astype(jnp.bfloat16)
    owner = owners[:, 0]
    hits = (owner[:, None] == jnp.arange(replicas, dtype=jnp.int32)[None, :]).astype(jnp.int32)
    before = jnp.cumsum(hits, axis=0) - hits
    slot_index = jnp.sum(before * hits, axis=1)
    target = owner * slots + slot_index
    placer = (jnp.arange(replicas * slots, dtype=jnp.int32)[:, None] == target[None, :]).astype(
        jnp.bfloat16
    )
    outgoing = jnp.dot(placer, masked, preferred_element_type=jnp.float32).astype(jnp.bfloat16)
    outgoing = outgoing.reshape(replicas, slots, columns)
    received = lax.all_to_all(outgoing, "dp", split_axis=0, concat_axis=0, tiled=True)
    values = received.astype(jnp.float32)
    square_sums = lax.psum(jnp.sum(values * values, axis=2), ("group", "section", "tensor"))
    scale = lax.rsqrt(square_sums / D + 1e-05)
    normed = (values * scale[:, :, None] * norm_gain[None, None, :]).astype(jnp.bfloat16)
    embedded = normed[None]
    grad_in = cotangent[0].astype(jnp.float32) * norm_gain[None, None, :]
    inner_sums = lax.psum(jnp.sum(grad_in * values, axis=2), ("group", "section", "tensor"))
    inner = inner_sums / D
    slot_grad = (scale[:, :, None] * grad_in - values * (scale**3 * inner)[:, :, None]).astype(
        jnp.bfloat16
    )
    returned = lax.all_to_all(slot_grad, "dp", split_axis=0, concat_axis=0, tiled=True)
    returned = returned.reshape(replicas * slots, columns)
    gathered = lax.dot_general(
        placer, returned, (((0,), (0,)), ((), ())), preferred_element_type=jnp.float32
    )
    back = (gathered * valid[:, None]).astype(jnp.bfloat16)
    input_terms = lax.dot_general(
        back, w_merge, (((1,), (1,)), ((), ())), preferred_element_type=jnp.float32
    )
    grad_merged = lax.psum_scatter(
        input_terms, ("group", "section", "tensor"), scatter_dimension=1, tiled=True
    )
    column_block = lax.all_to_all(merged, "dp", split_axis=1, concat_axis=0, tiled=True)
    grad_weight = lax.dot_general(
        column_block,
        lax.all_gather(back, "dp", axis=0, tiled=True),
        (((0,), (0,)), ((), ())),
        preferred_element_type=jnp.float32,
    )
    return (embedded, grad_merged, grad_weight)


def solution(mesh):
    placed = (
        P("dp", None),
        P("dp"),
        P("dp", None),
        P(None, ("group", "section", "tensor")),
        P(("group", "section", "tensor")),
        P("dp", None, None, ("group", "section", "tensor")),
    )
    return jax.shard_map(
        on_device,
        mesh=mesh,
        in_specs=placed,
        out_specs=(
            P("dp", None, None, ("group", "section", "tensor")),
            P("dp", ("group", "section", "tensor")),
            P("dp", ("group", "section", "tensor")),
        ),
        check_vma=False,
    )
```

profile of v0, /device:TPU:0, one launch (start us, length us, event | category | flops | bytes accessed | tf_op | source)
XLA Modules:
  0.0 182.4 jit_solution(6930971145670902794)
XLA Ops:
  8.0 0.0 all-gather.2.cloned.1.call-start
  8.1 0.7 iota_compare_fusion.3
  8.7 0.7 fusion.18
  9.5 1.2 reduce-window.6
  10.8 0.1 slice.12
  10.8 0.1 copy.23
  11.0 0.1 copy.24
  11.1 0.1 add_bitcast_fusion
  11.2 0.7 fusion.16
  11.9 0.7 multiply_add_fusion
  12.5 7.0 %convolution_convert_fusion = bf16[384,1024]{1,0:T(8,128)(2,1)S(1)} fusion(bf16[192,5120]{1,0:T(8,128)(2,1)} %param.6, bf16[5120,1024]{1,0:T(8,128)(2,1)} %param.9, f32[192]{0:T(256)S(1)} %compare_convert_fusion, s32[192]{0:T(256)S(1)} %multiply_add_fusion), kind=kOutput, calls=%fused_computation.14 | convolution fusion | flops 2165514240 | bytes 13239808 | tf_op jit(solution)/shard_map/dot_general | solution.py:31
  19.6 26.4 %all_to_all.29 = bf16[4,96,1024]{2,1,0:T(8,128)(2,1)S(1)} all-to-all(bf16[4,96,1024]{2,1,0:T(8,128)(2,1)S(1)} %bitcast.38), channel_id=1, replica_groups=mesh['group'=2,'dp'=4,'section'=2,'tensor'=2] {'dp'}, dimensions={0} | all-to-all | bytes 1572864 | tf_op jit(solution)/shard_map/all_to_all | solution.py:33
  46.0 0.4 fusion.3
  46.4 14.3 %all-reduce.1 = (f32[4,96]{1,0:T(4,128)S(1)}, f32[4,96]{1,0:T(4,128)S(1)}) all-reduce(f32[4,96]{1,0:T(4,128)S(1)} %get-tuple-element.19, f32[4,96]{1,0:T(4,128)S(1)} %get-tuple-element.18), channel_id=1, replica_groups=mesh['group'=2,'dp'=4,'section'=2,'tensor'=2] {'group','section','tensor'}, use_global_device_ids=true, to_apply=%region_5.6 | all-reduce | flops 768 | bytes 6144 | tf_op jit(solution)/shard_map/psum | solution.py:35
  60.7 1.4 fusion.5
  62.1 23.6 %all_to_all.30 = bf16[4,96,1024]{2,1,0:T(8,128)(2,1)S(1)} all-to-all(bf16[4,96,1024]{2,1,0:T(8,128)(2,1)S(1)} %get-tuple-element.22), channel_id=1, replica_groups=mesh['group'=2,'dp'=4,'section'=2,'tensor'=2] {'dp'}, dimensions={0} | all-to-all | bytes 1572864 | tf_op jit(solution)/shard_map/all_to_all | solution.py:45
  85.7 1.2 fusion.7
  86.9 0.0 reduce-scatter.2.cloned.1.call-start
  86.9 9.7 %fusion.21 = f32[192,5120]{1,0:T(8,128)} fusion(bf16[192,1024]{1,0:T(8,128)(2,1)} %fusion.7, bf16[5120,1024]{1,0:T(8,128)(2,1)} %param.9), kind=kOutput, calls=%fused_computation.48 | convolution fusion | flops 2013265920 | bytes 14811136 | tf_op jit(solution)/shard_map/dot_general | solution.py:51
  96.7 1.5 copy-done.1
  98.2 0.1 copy.31
  98.3 64.7 %all_to_all.31 = bf16[192,4,1280]{2,0,1:T(8,128)(2,1)S(1)} all-to-all(bf16[192,4,1280]{2,0,1:T(8,128)(2,1)S(1)} %bitcast.34), channel_id=1, replica_groups=mesh['group'=2,'dp'=4,'section'=2,'tensor'=2] {'dp'}, dimensions={1} | all-to-all | bytes 3932160 | tf_op jit(solution)/shard_map/all_to_all | solution.py:57
  163.1 6.0 %convolution_bitcast_fusion = f32[1280,1024]{0,1:T(8,128)} fusion(bf16[768,1024]{1,0:T(8,128)(2,1)} %all-gather.2.cloned.1.call-done, bf16[768,1280]{1,0:T(8,128)(2,1)S(1)} %bitcast.37), kind=kOutput, calls=%fused_computation | convolution fusion | flops 2013265920 | bytes 8781824 | tf_op jit(solution)/shard_map/dot_general | solution.py:58
  169.1 5.9 %copy.26 = f32[1280,1024]{1,0:T(8,128)} copy(f32[1280,1024]{0,1:T(8,128)} %convolution_bitcast_fusion) | data formatting | bytes 10485760
  (17 shorter events, 0.2 us)
Async XLA Ops:
  8.0 155.1 %all-gather.2.cloned.1.call-start = ((), (), s32[]{:S(2)}) async-start(), calls=%async_computation.5 | async-start | bytes 1966080 | tf_op jit(solution)/shard_map/all_gather | solution.py:60
  12.5 33.4 %copy-start.2 = (f32[1024]{0:T(1024)S(1)}, f32[1024]{0:T(1024)}, u32[]{:S(2)}) copy-start(f32[1024]{0:T(1024)} %param.10) | copy-start | bytes 12292
  19.6 26.4 %copy-start = (bf16[1,4,96,1024]{3,2,1,0:T(8,128)(2,1)S(1)}, bf16[1,4,96,1024]{3,2,1,0:T(8,128)(2,1)}, u32[]{:S(2)}) copy-start(bf16[1,4,96,1024]{3,2,1,0:T(8,128)(2,1)} %param.11) | copy-start | bytes 2359300
  86.9 88.1 %reduce-scatter.2.cloned.1.call-start = ((), (), s32[]{:S(2)}) async-start(), calls=%async_computation.4 | async-start | bytes 4423680 | tf_op jit(solution)/shard_map/reduce_scatter | solution.py:54
  96.7 1.5 copy-start.1
Sparse Core Ops, SparseCore 0:
  87.0 58.4 all-gather.1
Sparse Core Ops, SparseCore 1:
  96.8 46.7 reduce-scatter.1
where the time goes:
time: 183 us; the launch traced here: 182 us
  blocking collectives  129 us (70%)
  matrix products  23.9 us (13%)
  between operations  15.5 us (8%)
  local copies, waits for them, and re-layouts  7.84 us (4%)
  other arithmetic  6.04 us (3%)
    all_to_all x1, blocking collectives, on_device(): lax.all_to_all(merged, 'dp', split_axis=1, concat_axis=0, tiled=True)  64.7 us
    all_to_all x1, blocking collectives, on_device(): lax.all_to_all(outgoing, 'dp', split_axis=0, concat_axis=0, tiled=True)  26.4 us
    all_to_all x1, blocking collectives, on_device(): lax.all_to_all(slot_grad, 'dp', split_axis=0, concat_axis=0, tiled=True)  23.6 us
    psum x1, blocking collectives, on_device(): lax.psum(jnp.sum(values * values, axis=2), ('group', 'section', 'tensor'))  14.3 us
    dot_general x1, matrix products, on_device(): lax.dot_general(back, w_merge, (((1,), (1,)), ((), ())), preferred_elemen...  9.72 us
    unnamed x8, local copies, waits for them, and re-layouts  7.42 us
    dot_general x1, matrix products, on_device(): jnp.dot(placer, masked, preferred_element_type=jnp.float32)  7.02 us
    dot_general x1, matrix products, on_device(): lax.dot_general(column_block, lax.all_gather(back, 'dp', axis=0, tiled=Tr...  5.97 us
  transfers between devices with their start and end apart: 2, of which 0 were waited for; matrix products, arithmetic and copies ran while one was open for 12% of the time, Pallas kernels for 0%

commit v1 on v0

--- a/solution.py
+++ b/solution.py
@@ -32,7 +32,9 @@
     outgoing = outgoing.reshape(replicas, slots, columns)
     received = lax.all_to_all(outgoing, "dp", split_axis=0, concat_axis=0, tiled=True)
     values = received.astype(jnp.float32)
-    square_sums = lax.psum(jnp.sum(values * values, axis=2), ("group", "section", "tensor"))
+    square_sums = jnp.sum(values * values, axis=2)
+    for s in ("group", ("section", "tensor")):
+        square_sums = lax.psum(square_sums, s)
     scale = lax.rsqrt(square_sums / D + 1e-05)
     normed = (values * scale[:, :, None] * norm_gain[None, None, :]).astype(jnp.bfloat16)
     embedded = normed[None]

time: 183 us -> 193 us (1.055)
  blocking collectives: 129 us -> 140 us
    psum x1 -> x3, blocking collectives: 14.3 us -> 26.3 us  [the longest x1 14.3 us: on_device(): lax.psum(jnp.sum(grad_in * values, axis=2), ('group', 'section', 'tensor'))]
    all_to_all x1, blocking collectives: 23.6 us -> 21.1 us  [on_device(): lax.all_to_all(slot_grad, 'dp', split_axis=0, concat_axis=0, tiled=True)]
  transfers between devices with their start and end apart: 2 -> 2, of which waited for: 0 -> 0; matrix products, arithmetic and copies ran while one was open for 12% -> 11% of each run, Pallas kernels for 0% -> 0%
where the time goes in v1:
time: 193 us
  blocking collectives  140 us (73%)
  matrix products  23.8 us (12%)
  between operations  15.5 us (8%)
  local copies, waits for them, and re-layouts  7.84 us (4%)
  other arithmetic  6.04 us (3%)
    all_to_all x1, blocking collectives, on_device(): lax.all_to_all(merged, 'dp', split_axis=1, concat_axis=0, tiled=True)  65.8 us
    all_to_all x1, blocking collectives, on_device(): lax.all_to_all(outgoing, 'dp', split_axis=0, concat_axis=0, tiled=True)  26.4 us
    all_to_all x1, blocking collectives, on_device(): lax.all_to_all(slot_grad, 'dp', split_axis=0, concat_axis=0, tiled=True)  21.1 us
    psum x1, blocking collectives, on_device(): lax.psum(jnp.sum(grad_in * values, axis=2), ('group', 'section', 'tensor'))  14.3 us
    psum x2, blocking collectives, on_device(): square_sums = lax.psum(square_sums, s)  12.1 us
    dot_general x1, matrix products, on_device(): lax.dot_general(back, w_merge, (((1,), (1,)), ((), ())), preferred_elemen...  9.66 us
    unnamed x8, local copies, waits for them, and re-layouts  7.42 us
    dot_general x1, matrix products, on_device(): jnp.dot(placer, masked, preferred_element_type=jnp.float32)  7.02 us
  transfers between devices with their start and end apart: 2, of which 0 were waited for; matrix products, arithmetic and copies ran while one was open for 11% of the time, Pallas kernels for 0%

profile of v1, /device:TPU:0, one launch (start us, length us, event | category | flops | bytes accessed | tf_op | source)
XLA Modules:
  0.0 192.9 jit_solution(674671091930638997)
XLA Ops:
  8.1 0.7 iota_compare_fusion.3
  8.7 0.7 fusion.18
  9.5 1.2 reduce-window.6
  10.8 0.1 slice.12
  10.8 0.1 copy.23
  11.0 0.1 copy.24
  11.1 0.1 add_bitcast_fusion
  11.2 0.7 fusion.16
  11.9 0.7 multiply_add_fusion
  12.5 7.0 %convolution_convert_fusion = bf16[384,1024]{1,0:T(8,128)(2,1)S(1)} fusion(bf16[192,5120]{1,0:T(8,128)(2,1)} %param.6, bf16[5120,1024]{1,0:T(8,128)(2,1)} %param.9, f32[192]{0:T(256)S(1)} %compare_convert_fusion, s32[192]{0:T(256)S(1)} %multiply_add_fusion), kind=kOutput, calls=%fused_computation.14 | convolution fusion | flops 2165514240 | bytes 13239808 | tf_op jit(solution)/shard_map/dot_general | solution.py:31
  19.6 26.4 %all_to_all.29 = bf16[4,96,1024]{2,1,0:T(8,128)(2,1)S(1)} all-to-all(bf16[4,96,1024]{2,1,0:T(8,128)(2,1)S(1)} %bitcast.38), channel_id=1, replica_groups=mesh['group'=2,'dp'=4,'section'=2,'tensor'=2] {'dp'}, dimensions={0} | all-to-all | bytes 1572864 | tf_op jit(solution)/shard_map/all_to_all | solution.py:33
  46.0 0.4 fusion.3
  46.4 14.3 %psum.23 = f32[4,96]{1,0:T(4,128)S(1)} all-reduce(f32[4,96]{1,0:T(4,128)S(1)} %get-tuple-element.18), channel_id=1, replica_groups=mesh['group'=2,'dp'=4,'section'=2,'tensor'=2] {'group','section','tensor'}, use_global_device_ids=true, to_apply=%region_8.9 | all-reduce | flops 384 | bytes 3072 | tf_op jit(solution)/shard_map/psum | solution.py:42
  60.7 2.8 %psum.21 = f32[4,96]{1,0:T(4,128)S(1)} all-reduce(f32[4,96]{1,0:T(4,128)S(1)} %get-tuple-element.19), channel_id=1, replica_groups=mesh['group'=2,'dp'=4,'section'=2,'tensor'=2] {'group'}, use_global_device_ids=true, to_apply=%region_5.6 | all-reduce | flops 384 | bytes 3072 | tf_op jit(solution)/shard_map/psum | solution.py:37
  63.5 9.3 %psum.22 = f32[4,96]{1,0:T(4,128)S(1)} all-reduce(f32[4,96]{1,0:T(4,128)S(1)} %psum.21), channel_id=1, replica_groups=mesh['group'=2,'dp'=4,'section'=2,'tensor'=2] {'section','tensor'}, use_global_device_ids=true, to_apply=%region_6.7 | all-reduce | flops 384 | bytes 3072 | tf_op jit(solution)/shard_map/psum | solution.py:37
  72.8 1.4 fusion.5
  74.2 21.1 %all_to_all.30 = bf16[4,96,1024]{2,1,0:T(8,128)(2,1)S(1)} all-to-all(bf16[4,96,1024]{2,1,0:T(8,128)(2,1)S(1)} %get-tuple-element.20), channel_id=1, replica_groups=mesh['group'=2,'dp'=4,'section'=2,'tensor'=2] {'dp'}, dimensions={0} | all-to-all | bytes 1572864 | tf_op jit(solution)/shard_map/all_to_all | solution.py:47
  95.3 1.2 fusion.7
  96.5 9.7 %fusion.21 = f32[192,5120]{1,0:T(8,128)} fusion(bf16[192,1024]{1,0:T(8,128)(2,1)} %fusion.7, bf16[5120,1024]{1,0:T(8,128)(2,1)} %param.9), kind=kOutput, calls=%fused_computation.48 | convolution fusion | flops 2013265920 | bytes 14811136 | tf_op jit(solution)/shard_map/dot_general | solution.py:53
  106.2 1.5 copy-done.1
  107.7 0.1 copy.31
  107.8 65.8 %all_to_all.31 = bf16[192,4,1280]{2,0,1:T(8,128)(2,1)S(1)} all-to-all(bf16[192,4,1280]{2,0,1:T(8,128)(2,1)S(1)} %bitcast.34), channel_id=1, replica_groups=mesh['group'=2,'dp'=4,'section'=2,'tensor'=2] {'dp'}, dimensions={1} | all-to-all | bytes 3932160 | tf_op jit(solution)/shard_map/all_to_all | solution.py:59
  173.6 6.0 %convolution_bitcast_fusion = f32[1280,1024]{0,1:T(8,128)} fusion(bf16[768,1024]{1,0:T(8,128)(2,1)} %all-gather.2.cloned.1.call-done, bf16[768,1280]{1,0:T(8,128)(2,1)S(1)} %bitcast.37), kind=kOutput, calls=%fused_computation | convolution fusion | flops 2013265920 | bytes 8781824 | tf_op jit(solution)/shard_map/dot_general | solution.py:60
  179.6 5.9 %copy.26 = f32[1280,1024]{1,0:T(8,128)} copy(f32[1280,1024]{0,1:T(8,128)} %convolution_bitcast_fusion) | data formatting | bytes 10485760
  (19 shorter events, 0.2 us)
Async XLA Ops:
  8.0 165.6 %all-gather.2.cloned.1.call-start = ((), (), s32[]{:S(2)}) async-start(), calls=%async_computation.5 | async-start | bytes 1966080 | tf_op jit(solution)/shard_map/all_gather | solution.py:62
  12.5 33.4 %copy-start.2 = (f32[1024]{0:T(1024)S(1)}, f32[1024]{0:T(1024)}, u32[]{:S(2)}) copy-start(f32[1024]{0:T(1024)} %param.10) | copy-start | bytes 12292
  19.6 26.4 %copy-start = (bf16[1,4,96,1024]{3,2,1,0:T(8,128)(2,1)S(1)}, bf16[1,4,96,1024]{3,2,1,0:T(8,128)(2,1)}, u32[]{:S(2)}) copy-start(bf16[1,4,96,1024]{3,2,1,0:T(8,128)(2,1)} %param.11) | copy-start | bytes 2359300
  96.5 89.0 %reduce-scatter.2.cloned.1.call-start = ((), (), s32[]{:S(2)}) async-start(), calls=%async_computation.4 | async-start | bytes 4423680 | tf_op jit(solution)/shard_map/reduce_scatter | solution.py:56
  106.2 1.5 copy-start.1
Sparse Core Ops, SparseCore 0:
  96.6 61.3 all-gather.1
Sparse Core Ops, SparseCore 1:
  106.3 47.7 reduce-scatter.1
